TPU v7x, 32 devices: a whole 2x2x4 slice. The times are simulated.
32 devices in a mesh: row: 4 (over z), col: 8 (over y, x, core).
Axes of the slice: x: 2, y: 2, z: 4, core: 2. Of those that a mesh axis runs over, the one named last changes fastest.
Arguments:
- tokens: bfloat16 [512, 8192], P('col', 'row'), may hold values from -6 to 6
- w_gate: bfloat16 [8192, 16384], P('row', 'col'), may hold values from -0.09375 to 0.09375
- w_up: bfloat16 [8192, 16384], P('row', 'col'), may hold values from -0.09375 to 0.09375
- w_down: bfloat16 [16384, 8192], P('col', 'row'), may hold values from -0.0625 to 0.0625
- mask_in: int32 [64, 32], P('col', 'row'), may hold values 0 or 1
- mask_out: int32 [64, 32], P('col', 'row'), may hold values 0 or 1
- out_grad: bfloat16 [512, 8192], P('col', 'row'), may hold values from -6 to 6
Outputs:
- output: bfloat16 [512, 8192], P('col', 'row')
- tokens_grad: bfloat16 [512, 8192], P('col', 'row')
- gate_wgrad: bfloat16 [8192, 16384], P('row', 'col')
- up_wgrad: bfloat16 [8192, 16384], P('row', 'col')
- down_wgrad: bfloat16 [16384, 8192], P('col', 'row')
All inputs are finite; a program needn't handle non-finite values. No bound on the sum of `mask_in` or of `mask_out` on one device may be relied on, other than what follows from the above.
Results may differ from a plain program's by a relative error of at most 0.0049.
Values may be sent and summed in bfloat16 or wider, within the bound.
A program may use at most 128 MiB of HBM per device.

v0:
```python
import jax
import jax.numpy as jnp
from jax import lax
from jax.sharding import PartitionSpec as P

BLOCK = 256


def spread(mask_tile):
    return jnp.repeat(jnp.repeat(mask_tile.T, BLOCK, axis=0), BLOCK, axis=1)


def transposed_right(left, right):
    return lax.dot_general(
        left, right, (((1,), (1,)), ((), ())), preferred_element_type=jnp.float32
    )


def transposed_left(left, right):
    return lax.dot_general(
        left, right, (((0,), (0,)), ((), ())), preferred_element_type=jnp.float32
    )


def local(tokens, w_gate, w_up, w_down, mask_in, mask_out, out_grad):
    keep_in = spread(mask_in).astype(jnp.bfloat16)
    keep_out = spread(mask_out).T.astype(jnp.bfloat16)
    gate_masked = w_gate * keep_in
    up_masked = w_up * keep_in
    down_masked = w_down * keep_out
    hidden_width = w_gate.shape[1]
    x_panel = lax.all_gather(tokens, "col", axis=0, tiled=True)
    row_block = x_panel
    gate_part = jnp.dot(row_block, gate_masked, preferred_element_type=jnp.float32)
    up_part = jnp.dot(row_block, up_masked, preferred_element_type=jnp.float32)
    joined = lax.psum_scatter(
        jnp.concatenate([gate_part, up_part], axis=1), "row", scatter_dimension=0, tiled=True
    )
    gate = joined[:, :hidden_width]
    up = joined[:, hidden_width:]
    sigmoid_gate = jax.nn.sigmoid(gate)
    hidden_share = (gate * sigmoid_gate * up).astype(jnp.bfloat16)
    hidden_full = lax.all_gather(hidden_share, "row", axis=0, tiled=True)
    row_block = hidden_full
    output = lax.psum_scatter(
        jnp.dot(row_block, down_masked, preferred_element_type=jnp.float32),
        "col",
        scatter_dimension=0,
        tiled=True,
    ).astype(jnp.bfloat16)
    dy_panel = lax.all_gather(out_grad, "col", axis=0, tiled=True)
    down_wgrad = (transposed_left(hidden_full, dy_panel) * keep_out.astype(jnp.float32)).astype(
        jnp.bfloat16
    )
    row_block = dy_panel
    hidden_grad = lax.psum_scatter(
        transposed_right(row_block, down_masked), "row", scatter_dimension=0, tiled=True
    )
    up_grad = (hidden_grad * gate * sigmoid_gate).astype(jnp.bfloat16)
    gate_grad = (hidden_grad * up * sigmoid_gate * (1.0 + gate * (1.0 - sigmoid_gate))).astype(
        jnp.bfloat16
    )
    gate_full, up_full = (
        lax.all_gather(gate_grad, "row", axis=0, tiled=True),
        lax.all_gather(up_grad, "row", axis=0, tiled=True),
    )
    keep_wide = keep_in.astype(jnp.float32)
    gate_wgrad = (transposed_left(x_panel, gate_full) * keep_wide).astype(jnp.bfloat16)
    up_wgrad = (transposed_left(x_panel, up_full) * keep_wide).astype(jnp.bfloat16)
    tokens_grad = lax.psum_scatter(
        transposed_right(gate_full, gate_masked) + transposed_right(up_full, up_masked),
        "col",
        scatter_dimension=0,
        tiled=True,
    ).astype(jnp.bfloat16)
    return (output, tokens_grad, gate_wgrad, up_wgrad, down_wgrad)


def solution(mesh):
    placed = (
        P("col", "row"),
        P("row", "col"),
        P("row", "col"),
        P("col", "row"),
        P("col", "row"),
        P("col", "row"),
        P("col", "row"),
    )
    return jax.shard_map(
        local,
        mesh=mesh,
        in_specs=placed,
        out_specs=(
            P("col", "row"),
            P("col", "row"),
            P("row", "col"),
            P("row", "col"),
            P("col", "row"),
        ),
        check_vma=False,
    )
```

profile of v0, /device:TPU:0, one launch (start us, length us, event | category | flops | bytes accessed | tf_op | source)
XLA Modules:
  0.0 554.7 jit_solution(6437327898248120053)
XLA Ops:
  7.2 0.0 all-gather.10.cloned.1.call-start
  7.2 0.7 all-gather.10.cloned.1.call-update
  7.9 0.0 all-gather.6.cloned.1.call-start
  7.9 0.7 all-gather.6.cloned.1.call-update
  8.7 0.0 reduce-scatter.9.cloned.1.call-start
  8.7 0.7 convert_bitcast_fusion
  9.4 0.1 copy.15
  9.5 0.1 broadcast_in_dim.14
  9.6 7.3 %bitcast_multiply_fusion.2 = bf16[2048,2048]{1,0:T(8,128)(2,1)} fusion(bf16[2048,2048]{1,0:T(8,128)(2,1)} %param.10, bf16[2048,8]{0,1:T(8,128)(2,1)S(1)} %bitcast.48), kind=kLoop, calls=%fused_computation.7 | loop fusion | flops 4194304 | bytes 16809984 | tf_op jit(solution)/shard_map/mul | solution.py:30
  16.9 23.5 %all-gather.10.cloned.1.call-done = bf16[512,2048]{1,0:T(8,128)(2,1)} async-done(((bf16[64,2048]{1,0:T(8,128)(2,1)}), bf16[512,2048]{1,0:T(8,128)(2,1)}) %all-gather.10.cloned.1.call-update) | async-done | bytes 2097168 | tf_op jit(solution)/shard_map/all_gather | solution.py:51
  40.4 10.5 %convolution_bitcast_fusion = f32[512,2048]{0,1:T(8,128)} fusion(bf16[2048,2048]{1,0:T(8,128)(2,1)} %bitcast_multiply_fusion.2, bf16[512,2048]{1,0:T(8,128)(2,1)} %all-gather.10.cloned.1.call-done), kind=kOutput, calls=%fused_computation.9 | convolution fusion | flops 4294967296 | bytes 14680064 | tf_op jit(solution)/shard_map/dot_general | solution.py:14
  50.9 0.0 reduce-scatter.9.cloned.1.call-update
  50.9 0.2 reduce-scatter.5.cloned.1.call-start
  51.2 0.4 copy-done.2
  51.6 0.1 copy.12
  51.7 12.2 %copy.13 = bf16[2048,2048]{0,1:T(8,128)(2,1)} copy(bf16[2048,2048]{1,0:T(8,128)(2,1)} %param.8) | data formatting | bytes 16777216 | tf_op args[1]
  63.9 12.2 %copy.14 = bf16[2048,2048]{0,1:T(8,128)(2,1)} copy(bf16[2048,2048]{1,0:T(8,128)(2,1)} %param.9) | data formatting | bytes 16777216 | tf_op args[2]
  76.2 0.1 broadcast_in_dim.12
  76.2 13.7 %bitcast_multiply_fusion.1 = (bf16[2048,2048]{0,1:T(8,128)(2,1)}, bf16[2048,2048]{0,1:T(8,128)(2,1)}) fusion(bf16[2048,2048]{0,1:T(8,128)(2,1)} %copy.13, bf16[2048,8]{0,1:T(8,128)(2,1)S(1)} %bitcast.50, bf16[2048,2048]{0,1:T(8,128)(2,1)} %copy.14), kind=kLoop, calls=%fused_computation.3 | loop fusion | flops 8388608 | bytes 33587200 | tf_op jit(solution)/shard_map/mul | solution.py:28
  89.9 7.8 %convolution_bitcast_fusion.1 = f32[512,2048]{0,1:T(8,128)S(1)} fusion(bf16[2048,2048]{0,1:T(8,128)(2,1)} %get-tuple-element.14, bf16[512,2048]{1,0:T(8,128)(2,1)} %all-gather.6.cloned.1.call-done), kind=kOutput, calls=%fused_computation.10 | convolution fusion | flops 4294967296 | bytes 14680064 | tf_op jit(solution)/shard_map/dot_general | solution.py:35
  97.7 4.8 convolution_bitcast_fusion.2
  102.5 4.2 pad_maximum_fusion
  106.8 0.0 reduce-scatter.5.cloned.1.call-update
  106.8 0.0 all-gather.12.cloned.1.call-start
  106.8 42.4 %reduce-scatter.9.cloned.1.call-done = f32[128,2048]{0,1:T(8,128)} async-done(((f32[512,2048]{0,1:T(8,128)}), f32[128,2048]{0,1:T(8,128)}) %reduce-scatter.9.cloned.1.call-update) | async-done | bytes 1048592 | tf_op jit(solution)/shard_map/reduce_scatter | solution.py:56
  149.2 147.4 %reduce-scatter.5.cloned.1.call-done = f32[128,4096]{0,1:T(8,128)} async-done(((f32[512,4096]{0,1:T(8,128)}), f32[128,4096]{0,1:T(8,128)}) %reduce-scatter.5.cloned.1.call-update) | async-done | bytes 2097168 | tf_op jit(solution)/shard_map/reduce_scatter | solution.py:36
  296.6 3.5 multiply_convert_fusion.1
  300.1 0.0 all-gather.12.cloned.1.call-update
  300.1 0.0 all-gather.14.cloned.1.call-start
  300.2 0.5 all-gather.14.cloned.1.call-update
  300.7 0.0 all-gather.8.cloned.1.call-start
  300.7 0.7 all-gather.8.cloned.1.call-update
  301.4 0.3 reduce-scatter.11.cloned.1.call-start
  301.7 45.4 %all-gather.12.cloned.1.call-done = bf16[512,2048]{0,1:T(8,128)(2,1)} async-done(((bf16[128,2048]{0,1:T(8,128)(2,1)}), bf16[512,2048]{0,1:T(8,128)(2,1)}) %all-gather.12.cloned.1.call-update) | async-done | bytes 2097168 | tf_op jit(solution)/shard_map/all_gather | solution.py:64
  347.1 10.6 %fusion.3 = f32[512,2048]{1,0:T(8,128)} fusion(bf16[512,2048]{0,1:T(8,128)(2,1)} %all-gather.12.cloned.1.call-done, bf16[2048,2048]{0,1:T(8,128)(2,1)} %get-tuple-element.13), kind=kOutput, calls=%fused_computation.20 | convolution fusion | flops 4294967296 | bytes 14680064 | tf_op jit(solution)/shard_map/dot_general | solution.py:14
  357.7 35.3 %all-gather.14.cloned.1.call-done = bf16[512,2048]{0,1:T(8,128)(2,1)} async-done(((bf16[128,2048]{0,1:T(8,128)(2,1)}), bf16[512,2048]{0,1:T(8,128)(2,1)}) %all-gather.14.cloned.1.call-update) | async-done | bytes 2097168 | tf_op jit(solution)/shard_map/all_gather | solution.py:65
  393.0 11.7 %convolution_add_fusion = f32[512,2048]{1,0:T(8,128)} fusion(f32[512,2048]{1,0:T(8,128)} %fusion.3, bf16[512,2048]{0,1:T(8,128)(2,1)} %all-gather.14.cloned.1.call-done, bf16[2048,2048]{0,1:T(8,128)(2,1)} %get-tuple-element.14), kind=kOutput, calls=%fused_computation.12 | convolution fusion | flops 4296015872 | bytes 18874368 | tf_op jit(solution)/shard_map/dot_general | solution.py:14
  404.8 0.3 reduce-scatter.7.cloned.1.call-start
  405.1 34.0 %all-gather.8.cloned.1.call-done = bf16[512,2048]{0,1:T(8,128)(2,1)} async-done(((bf16[128,2048]{0,1:T(8,128)(2,1)}), bf16[512,2048]{0,1:T(8,128)(2,1)}) %all-gather.8.cloned.1.call-update) | async-done | bytes 2097168 | tf_op jit(solution)/shard_map/all_gather | solution.py:43
  439.1 10.5 %fusion.2 = f32[512,2048]{1,0:T(8,128)} fusion(bf16[512,2048]{0,1:T(8,128)(2,1)} %all-gather.8.cloned.1.call-done, bf16[2048,2048]{1,0:T(8,128)(2,1)} %bitcast_multiply_fusion.2), kind=kOutput, calls=%fused_computation.19 | convolution fusion | flops 4294967296 | bytes 14680064 | tf_op jit(solution)/shard_map/dot_general | solution.py:46
  449.6 8.5 %fusion = bf16[2048,2048]{0,1:T(8,128)(2,1)} fusion(bf16[512,2048]{0,1:T(8,128)(2,1)} %all-gather.12.cloned.1.call-done, bf16[512,2048]{1,0:T(8,128)(2,1)S(1)} %copy-done.4, bf16[2048,8]{0,1:T(8,128)(2,1)S(1)} %bitcast.51), kind=kOutput, calls=%fused_computation.4 | convolution fusion | flops 4307550208 | bytes 12615680 | tf_op jit(solution)/shard_map/dot_general | solution.py:20
  458.1 12.0 %copy.16 = bf16[2048,2048]{1,0:T(8,128)(2,1)} copy(bf16[2048,2048]{0,1:T(8,128)(2,1)} %fusion) | data formatting | bytes 16777216
  470.1 8.3 %fusion.1 = bf16[2048,2048]{0,1:T(8,128)(2,1)} fusion(bf16[512,2048]{0,1:T(8,128)(2,1)S(1)} %copy-done.1, bf16[512,2048]{1,0:T(8,128)(2,1)} %all-gather.6.cloned.1.call-done, bf16[2048,8]{0,1:T(8,128)(2,1)S(1)} %bitcast.52), kind=kOutput, calls=%fused_computation.5 | convolution fusion | flops 4307550208 | bytes 12615680 | tf_op jit(solution)/shard_map/dot_general | solution.py:20
  478.4 12.4 %copy.17 = bf16[2048,2048]{1,0:T(8,128)(2,1)} copy(bf16[2048,2048]{0,1:T(8,128)(2,1)} %fusion.1) | data formatting | bytes 16777216
  490.8 8.4 %multiply_convert_fusion = bf16[2048,2048]{1,0:T(8,128)(2,1)} fusion(bf16[512,2048]{0,1:T(8,128)(2,1)} %all-gather.8.cloned.1.call-done, bf16[512,2048]{1,0:T(8,128)(2,1)S(1)} %copy-done.3, bf16[2048,8]{0,1:T(8,128)(2,1)S(1)} %bitcast.49), kind=kOutput, calls=%fused_computation.6 | convolution fusion | flops 4307550208 | bytes 12615680 | tf_op jit(solution)/shard_map/dot_general | solution.py:20
  499.2 1.8 convert_element_type.74
  501.0 45.4 %reduce-scatter.7.cloned.1.call-done = f32[64,2048]{1,0:T(8,128)} async-done(((f32[512,2048]{1,0:T(8,128)}), f32[64,2048]{1,0:T(8,128)}) %reduce-scatter.7.cloned.1.call-update) | async-done | bytes 524304 | tf_op jit(solution)/shard_map/reduce_scatter | solution.py:45
  546.4 1.8 convert_element_type.71
  (14 shorter events, 0.1 us)
Async XLA Ops:
  7.2 33.2 %all-gather.10.cloned.1.call-start = ((), (), s32[]{:S(2)}) async-start(), calls=%async_computation.8 | async-start | bytes 2359296 | tf_op jit(solution)/shard_map/all_gather | solution.py:51
  7.9 82.0 %all-gather.6.cloned.1.call-start = ((), (), s32[]{:S(2)}) async-start(), calls=%async_computation.4 | async-start | bytes 2359296 | tf_op jit(solution)/shard_map/all_gather | solution.py:32
  8.7 140.6 %reduce-scatter.9.cloned.1.call-start = ((), (), s32[]{:S(2)}) async-start(), calls=%async_computation.9 | async-start | bytes 5242880 | tf_op jit(solution)/shard_map/reduce_scatter | solution.py:56
  50.9 0.7 copy-start.2
  50.9 245.6 %reduce-scatter.5.cloned.1.call-start = ((), (), s32[]{:S(2)}) async-start(), calls=%async_computation.5 | async-start | bytes 10485760 | tf_op jit(solution)/shard_map/reduce_scatter | solution.py:36
  89.9 7.8 %copy-start = (bf16[2048,2048]{0,1:T(8,128)(2,1)S(1)}, bf16[2048,2048]{0,1:T(8,128)(2,1)}, u32[]{:S(2)}) copy-start(bf16[2048,2048]{0,1:T(8,128)(2,1)} %get-tuple-element.13) | copy-start | bytes 25165828
  89.9 7.8 %copy-start.4 = (bf16[512,2048]{1,0:T(8,128)(2,1)S(1)}, bf16[512,2048]{1,0:T(8,128)(2,1)}, u32[]{:S(2)}) copy-start(bf16[512,2048]{1,0:T(8,128)(2,1)} %all-gather.6.cloned.1.call-done) | copy-start | bytes 6291460
  106.8 240.4 %all-gather.12.cloned.1.call-start = ((), (), s32[]{:S(2)}) async-start(), calls=%async_computation.10 | async-start | bytes 2621440 | tf_op jit(solution)/shard_map/all_gather | solution.py:64
  300.1 92.9 %all-gather.14.cloned.1.call-start = ((), (), s32[]{:S(2)}) async-start(), calls=%async_computation.11 | async-start | bytes 2621440 | tf_op jit(solution)/shard_map/all_gather | solution.py:65
  300.7 138.4 %all-gather.8.cloned.1.call-start = ((), (), s32[]{:S(2)}) async-start(), calls=%async_computation.6 | async-start | bytes 2621440 | tf_op jit(solution)/shard_map/all_gather | solution.py:43
  301.4 197.7 %reduce-scatter.11.cloned.1.call-start = ((), (), s32[]{:S(2)}) async-start(), calls=%async_computation.12 | async-start | bytes 4718592 | tf_op jit(solution)/shard_map/reduce_scatter | solution.py:70
  404.8 141.6 %reduce-scatter.7.cloned.1.call-start = ((), (), s32[]{:S(2)}) async-start(), calls=%async_computation.7 | async-start | bytes 4718592 | tf_op jit(solution)/shard_map/reduce_scatter | solution.py:45
  458.1 12.0 %copy-start.1 = (bf16[512,2048]{0,1:T(8,128)(2,1)S(1)}, bf16[512,2048]{0,1:T(8,128)(2,1)}, u32[]{:S(2)}) copy-start(bf16[512,2048]{0,1:T(8,128)(2,1)} %all-gather.14.cloned.1.call-done) | copy-start | bytes 6291460
  478.4 12.4 %copy-start.3 = (bf16[512,2048]{1,0:T(8,128)(2,1)S(1)}, bf16[512,2048]{1,0:T(8,128)(2,1)}, u32[]{:S(2)}) copy-start(bf16[512,2048]{1,0:T(8,128)(2,1)} %all-gather.10.cloned.1.call-done) | copy-start | bytes 6291460
Sparse Core Ops, SparseCore 0:
  9.9 30.4 all-gather.9
  42.3 27.7 all-gather.5
  72.4 76.7 reduce-scatter.8
  151.4 145.1 reduce-scatter.4
  300.2 46.8 all-gather.11
  348.6 44.4 all-gather.13
  394.6 44.4 all-gather.7
  442.4 49.3 reduce-scatter.10
  495.2 51.1 reduce-scatter.6
where the time goes:
time: 556 us; the launch traced here: 555 us
  waiting for transfers between devices  376 us (68%)
  matrix products  81.1 us (15%)
  local copies, waits for them, and re-layouts  49.6 us (9%)
  other arithmetic  33 us (6%)
  between operations  13.9 us (2%)
    reduce_scatter x1, waiting for transfers between devices, local(): lax.psum_scatter(jnp.concatenate([gate_part, up_part], axis=1), 'row', sc...  147 us
    unnamed x14, local copies, waits for them, and re-layouts  49.3 us
    all_gather x1, waiting for transfers between devices, local(): lax.all_gather(gate_grad, 'row', axis=0, tiled=True)  45.4 us
    reduce_scatter x1, waiting for transfers between devices, local(): lax.psum_scatter(jnp.dot(row_block, down_masked, preferred_element_type=j...  45.4 us
    reduce_scatter x1, waiting for transfers between devices, local(): lax.psum_scatter(transposed_right(row_block, down_masked), 'row', scatter...  42.4 us
    all_gather x1, waiting for transfers between devices, local(): lax.all_gather(up_grad, 'row', axis=0, tiled=True)  35.3 us
    all_gather x1, waiting for transfers between devices, local(): hidden_full = lax.all_gather(hidden_share, 'row', axis=0, tiled=True)  34 us
    dot_general x3, matrix products, transposed_right(): lax.dot_general(left, right, (((1,), (1,)), ((), ())), preferred_element_...  32.8 us
  transfers between devices with their start and end apart: 9, of which 7 were waited for; matrix products, arithmetic and copies ran while one was open for 28% of the time, Pallas kernels for 0%

commit v1 on v0

--- a/solution.py
+++ b/solution.py
@@ -4,6 +4,22 @@
 from jax.sharding import PartitionSpec as P
 
 BLOCK = 256
+
+
+def write_gates(inp, row_axis):
+    extent = lax.axis_size(row_axis)
+    line_up = [(it, (it + 1) % extent) for it in range(extent)]
+
+    def circles_replace(tall):
+        if len(tall) == extent:
+            return tall
+        outcome_arr = lax.ppermute(tall[0], row_axis, line_up)
+        return circles_replace([outcome_arr, *tall])
+
+    z = circles_replace([inp])
+    v_next = jnp.concatenate(z, 0)
+    state_next = lax.axis_index(row_axis)
+    return jnp.roll(v_next, (state_next + 1) * inp.shape[0], 0)
 
 
 def spread(mask_tile):
@@ -40,7 +56,7 @@
     up = joined[:, hidden_width:]
     sigmoid_gate = jax.nn.sigmoid(gate)
     hidden_share = (gate * sigmoid_gate * up).astype(jnp.bfloat16)
-    hidden_full = lax.all_gather(hidden_share, "row", axis=0, tiled=True)
+    hidden_full = write_gates(hidden_share, "row")
     row_block = hidden_full
     output = lax.psum_scatter(
         jnp.dot(row_block, down_masked, preferred_element_type=jnp.float32),

time: 556 us -> 527 us (0.948)
  waiting for transfers between devices: 376 us -> 328 us
  starting transfers between devices: 1.02 us -> 17 us
    ppermute x0 -> x3, waiting for transfers between devices: none -> 54.8 us  [circles_replace(): outcome_arr = lax.ppermute(tall[0], row_axis, line_up)]
    reduce_scatter x1, waiting for transfers between devices: 45.4 us -> 0.01 us  [local(): lax.psum_scatter(jnp.dot(row_block, down_masked, preferred_element_type=j...]
    all_gather x1, waiting for transfers between devices: 45.4 us -> 0.02 us  [local(): lax.all_gather(gate_grad, 'row', axis=0, tiled=True)]
    reduce_scatter x1, waiting for transfers between devices: 0.01 us -> 43.7 us  [local(): lax.psum_scatter(transposed_right(gate_full, gate_masked) + transposed_ri...]
    all_gather x1 -> x0, waiting for transfers between devices: 34 us -> none  [local(): hidden_full = lax.all_gather(hidden_share, 'row', axis=0, tiled=True)]
    all_gather x1, waiting for transfers between devices: 35.3 us -> 14.9 us  [local(): lax.all_gather(up_grad, 'row', axis=0, tiled=True)]
    ppermute x0 -> x3, starting transfers between devices: none -> 16.3 us  [circles_replace(): outcome_arr = lax.ppermute(tall[0], row_axis, line_up)]
    unnamed x14 -> x27, local copies, waits for them, and re-layouts: 49.3 us -> 54.5 us
  transfers between devices with their start and end apart: 9 -> 11, of which waited for: 7 -> 8; matrix products, arithmetic and copies ran while one was open for 28% -> 30% of each run, Pallas kernels for 0% -> 0%
where the time goes in v1:
time: 527 us; the launch traced here: 526 us
  waiting for transfers between devices  328 us (62%)
  matrix products  78.6 us (15%)
  local copies, waits for them, and re-layouts  55 us (10%)
  other arithmetic  32.9 us (6%)
  starting transfers between devices  17 us (3%)
  between operations  14.3 us (3%)
    reduce_scatter x1, waiting for transfers between devices, local(): lax.psum_scatter(jnp.concatenate([gate_part, up_part], axis=1), 'row', sc...  147 us
    ppermute x3, waiting for transfers between devices, circles_replace(): outcome_arr = lax.ppermute(tall[0], row_axis, line_up)  54.8 us
    unnamed x27, local copies, waits for them, and re-layouts  54.5 us
    reduce_scatter x1, waiting for transfers between devices, local(): lax.psum_scatter(transposed_right(gate_full, gate_masked) + transposed_ri...  43.7 us
    reduce_scatter x1, waiting for transfers between devices, local(): lax.psum_scatter(transposed_right(row_block, down_masked), 'row', scatter...  42.4 us
    dot_general x3, matrix products, transposed_right(): lax.dot_general(left, right, (((1,), (1,)), ((), ())), preferred_element_...  32.8 us
    dot_general x3, matrix products, transposed_left(): lax.dot_general(left, right, (((0,), (0,)), ((), ())), preferred_element_...  23.7 us
    all_gather x1, waiting for transfers between devices, local(): dy_panel = lax.all_gather(out_grad, 'col', axis=0, tiled=True)  23.5 us
  transfers between devices with their start and end apart: 11, of which 8 were waited for; matrix products, arithmetic and copies ran while one was open for 30% of the time, Pallas kernels for 0%

profile of v1, /device:TPU:0, one launch (start us, length us, event | category | flops | bytes accessed | tf_op | source)
XLA Modules:
  0.0 525.9 jit_solution(6620633989236931014)
XLA Ops:
  7.2 0.7 all-gather.7.cloned.1.call-update
  7.9 0.7 all-gather.5.cloned.1.call-update
  8.7 0.7 convert_bitcast_fusion
  9.4 0.1 copy.15
  9.6 7.3 %bitcast_multiply_fusion.2 = bf16[2048,2048]{1,0:T(8,128)(2,1)} fusion(bf16[2048,2048]{1,0:T(8,128)(2,1)} %param.10, bf16[2048,8]{0,1:T(8,128)(2,1)S(1)} %bitcast.46), kind=kLoop, calls=%fused_computation.7 | loop fusion | flops 4194304 | bytes 16809984 | tf_op jit(solution)/shard_map/mul | solution.py:46
  16.9 23.5 %all-gather.7.cloned.1.call-done = bf16[512,2048]{1,0:T(8,128)(2,1)} async-done(((bf16[64,2048]{1,0:T(8,128)(2,1)}), bf16[512,2048]{1,0:T(8,128)(2,1)}) %all-gather.7.cloned.1.call-update) | async-done | bytes 2097168 | tf_op jit(solution)/shard_map/all_gather | solution.py:67
  40.4 10.5 %convolution_bitcast_fusion = f32[512,2048]{0,1:T(8,128)} fusion(bf16[2048,2048]{1,0:T(8,128)(2,1)} %bitcast_multiply_fusion.2, bf16[512,2048]{1,0:T(8,128)(2,1)} %all-gather.7.cloned.1.call-done), kind=kOutput, calls=%fused_computation.9 | convolution fusion | flops 4294967296 | bytes 14680064 | tf_op jit(solution)/shard_map/dot_general | solution.py:30
  50.9 0.2 reduce-scatter.5.cloned.1.call-start
  51.2 0.4 copy-done.3
  51.6 0.1 copy.12
  51.7 12.2 %copy.13 = bf16[2048,2048]{0,1:T(8,128)(2,1)} copy(bf16[2048,2048]{1,0:T(8,128)(2,1)} %param.8) | data formatting | bytes 16777216 | tf_op args[1]
  63.9 12.2 %copy.14 = bf16[2048,2048]{0,1:T(8,128)(2,1)} copy(bf16[2048,2048]{1,0:T(8,128)(2,1)} %param.9) | data formatting | bytes 16777216 | tf_op args[2]
  76.2 13.7 %bitcast_multiply_fusion.1 = (bf16[2048,2048]{0,1:T(8,128)(2,1)}, bf16[2048,2048]{0,1:T(8,128)(2,1)}) fusion(bf16[2048,2048]{0,1:T(8,128)(2,1)} %copy.13, bf16[2048,8]{0,1:T(8,128)(2,1)S(1)} %bitcast.48, bf16[2048,2048]{0,1:T(8,128)(2,1)} %copy.14), kind=kLoop, calls=%fused_computation.3 | loop fusion | flops 8388608 | bytes 33587200 | tf_op jit(solution)/shard_map/mul | solution.py:44
  89.9 7.8 %convolution_bitcast_fusion.1 = f32[512,2048]{0,1:T(8,128)S(1)} fusion(bf16[2048,2048]{0,1:T(8,128)(2,1)} %get-tuple-element.14, bf16[512,2048]{1,0:T(8,128)(2,1)} %all-gather.5.cloned.1.call-done), kind=kOutput, calls=%fused_computation.10 | convolution fusion | flops 4294967296 | bytes 14680064 | tf_op jit(solution)/shard_map/dot_general | solution.py:51
  97.7 4.8 convolution_bitcast_fusion.2
  102.5 4.2 pad_maximum_fusion
  106.8 42.4 %reduce-scatter.9.cloned.1.call-done = f32[128,2048]{0,1:T(8,128)} async-done(((f32[512,2048]{0,1:T(8,128)}), f32[128,2048]{0,1:T(8,128)}) %reduce-scatter.9.cloned.1.call-update) | async-done | bytes 1048592 | tf_op jit(solution)/shard_map/reduce_scatter | solution.py:72
  149.2 147.4 %reduce-scatter.5.cloned.1.call-done = f32[128,4096]{0,1:T(8,128)} async-done(((f32[512,4096]{0,1:T(8,128)}), f32[128,4096]{0,1:T(8,128)}) %reduce-scatter.5.cloned.1.call-update) | async-done | bytes 2097168 | tf_op jit(solution)/shard_map/reduce_scatter | solution.py:52
  296.6 3.4 multiply_convert_fusion.1
  300.1 1.1 collective-permute-start
  301.2 17.8 %collective-permute-done = bf16[128,2048]{0,1:T(8,128)(2,1)S(1)} collective-permute-done((bf16[128,2048]{0,1:T(8,128)(2,1)S(1)}, bf16[128,2048]{0,1:T(8,128)(2,1)S(1)}, u32[]{:S(2)}, u32[]{:S(2)}) %collective-permute-start) | collective-permute-done | bytes 524320 | tf_op jit(solution)/shard_map/ppermute | solution.py:16
  319.0 6.7 %collective-permute-start.1 = (bf16[128,2048]{0,1:T(8,128)(2,1)S(1)}, bf16[128,2048]{0,1:T(8,128)(2,1)S(1)}, u32[]{:S(2)}, u32[]{:S(2)}) collective-permute-start(bf16[128,2048]{0,1:T(8,128)(2,1)S(1)} %collective-permute-done), channel_id=1, source_target_pairs={{0,8},{8,16},{16,24},{24,0},{1,9},{9,17},{17,25},{25,1},{2,10},{10... | collective-permute-start | bytes 1572872 | tf_op jit(solution)/shard_map/ppermute | solution.py:16
  325.7 22.1 %collective-permute-done.1 = bf16[128,2048]{0,1:T(8,128)(2,1)S(1)} collective-permute-done((bf16[128,2048]{0,1:T(8,128)(2,1)S(1)}, bf16[128,2048]{0,1:T(8,128)(2,1)S(1)}, u32[]{:S(2)}, u32[]{:S(2)}) %collective-permute-start.1) | collective-permute-done | bytes 524320 | tf_op jit(solution)/shard_map/ppermute | solution.py:16
  347.8 8.5 %collective-permute-start.2 = (bf16[128,2048]{0,1:T(8,128)(2,1)S(1)}, bf16[128,2048]{0,1:T(8,128)(2,1)S(1)}, u32[]{:S(2)}, u32[]{:S(2)}) collective-permute-start(bf16[128,2048]{0,1:T(8,128)(2,1)S(1)} %collective-permute-done.1), channel_id=1, source_target_pairs={{0,8},{8,16},{16,24},{24,0},{1,9},{9,17},{17,25},{25,1},{2,10},{10... | collective-permute-start | bytes 1572872 | tf_op jit(solution)/shard_map/ppermute | solution.py:16
  356.4 0.3 reduce-scatter.7.cloned.1.call-start
  356.7 14.8 %collective-permute-done.2 = bf16[128,2048]{0,1:T(8,128)(2,1)S(1)} collective-permute-done((bf16[128,2048]{0,1:T(8,128)(2,1)S(1)}, bf16[128,2048]{0,1:T(8,128)(2,1)S(1)}, u32[]{:S(2)}, u32[]{:S(2)}) %collective-permute-start.2) | collective-permute-done | bytes 524320 | tf_op jit(solution)/shard_map/ppermute | solution.py:16
  371.5 0.1 constant_dynamic-update-slice_fusion.7
  371.6 0.2 constant_dynamic-update-slice_fusion.6
  371.8 0.2 constant_dynamic-update-slice_fusion.5
  372.0 0.2 constant_dynamic-update-slice_fusion.4
  372.2 0.2 constant_dynamic-update-slice_fusion.3
  372.4 0.2 constant_dynamic-update-slice_fusion.2
  372.6 0.2 constant_dynamic-update-slice_fusion.1
  372.8 0.2 constant_dynamic-update-slice_fusion
  373.0 1.9 copy-done.2
  374.9 9.5 %fusion.3 = f32[512,2048]{1,0:T(8,128)} fusion(bf16[2048,2048]{1,0:T(8,128)(2,1)} %bitcast_multiply_fusion.2, bf16[1024,2048]{0,1:T(8,128)(2,1)S(1)} %constant_dynamic-update-slice_fusion, s32[]{:T(128)S(6)} %select_n.14), kind=kOutput, calls=%fused_computation.14 | convolution fusion | flops 4294967296 | bytes 14680068 | tf_op jit(solution)/shard_map/dot_general | solution.py:62
  384.5 10.6 %fusion.7 = f32[512,2048]{1,0:T(8,128)} fusion(bf16[512,2048]{0,1:T(8,128)(2,1)} %all-gather.9.cloned.1.call-done, bf16[2048,2048]{0,1:T(8,128)(2,1)} %get-tuple-element.13), kind=kOutput, calls=%fused_computation.32 | convolution fusion | flops 4294967296 | bytes 14680064 | tf_op jit(solution)/shard_map/dot_general | solution.py:30
  395.1 14.9 %all-gather.11.cloned.1.call-done = bf16[512,2048]{0,1:T(8,128)(2,1)} async-done(((bf16[128,2048]{0,1:T(8,128)(2,1)}), bf16[512,2048]{0,1:T(8,128)(2,1)}) %all-gather.11.cloned.1.call-update) | async-done | bytes 2097168 | tf_op jit(solution)/shard_map/all_gather | solution.py:81
  410.0 11.7 %convolution_add_fusion = f32[512,2048]{1,0:T(8,128)} fusion(f32[512,2048]{1,0:T(8,128)} %fusion.7, bf16[512,2048]{0,1:T(8,128)(2,1)} %all-gather.11.cloned.1.call-done, bf16[2048,2048]{0,1:T(8,128)(2,1)} %get-tuple-element.14), kind=kOutput, calls=%fused_computation.12 | convolution fusion | flops 4296015872 | bytes 18874368 | tf_op jit(solution)/shard_map/dot_general | solution.py:30
  421.7 1.8 copy-done.6
  423.5 8.6 %multiply_convert_fusion = bf16[2048,2048]{1,0:T(8,128)(2,1)} fusion(bf16[512,2048]{1,0:T(8,128)(2,1)S(1)} %copy-done.6, bf16[2048,8]{0,1:T(8,128)(2,1)S(1)} %bitcast.47, bf16[1024,2048]{0,1:T(8,128)(2,1)} %copy-done.2, s32[]{:T(128)S(6)} %select_n.14), kind=kOutput, calls=%fused_computation.6 | convolution fusion | flops 4307550208 | bytes 12615684 | tf_op jit(solution)/shard_map/dot_general | solution.py:36
  432.1 6.8 %fusion = bf16[2048,2048]{0,1:T(8,128)(2,1)} fusion(bf16[512,2048]{0,1:T(8,128)(2,1)S(1)} %copy-done.7, bf16[512,2048]{1,0:T(8,128)(2,1)S(1)} %copy-done.5, bf16[2048,8]{0,1:T(8,128)(2,1)S(1)} %bitcast.49), kind=kOutput, calls=%fused_computation.4 | convolution fusion | flops 4307550208 | bytes 12615680 | tf_op jit(solution)/shard_map/dot_general | solution.py:36
  438.9 12.4 %copy.16 = bf16[2048,2048]{1,0:T(8,128)(2,1)} copy(bf16[2048,2048]{0,1:T(8,128)(2,1)} %fusion) | data formatting | bytes 16777216
  451.3 8.3 %fusion.1 = bf16[2048,2048]{0,1:T(8,128)(2,1)} fusion(bf16[512,2048]{0,1:T(8,128)(2,1)S(1)} %copy-done.1, bf16[512,2048]{1,0:T(8,128)(2,1)} %all-gather.5.cloned.1.call-done, bf16[2048,8]{0,1:T(8,128)(2,1)S(1)} %bitcast.50), kind=kOutput, calls=%fused_computation.5 | convolution fusion | flops 4307550208 | bytes 12615680 | tf_op jit(solution)/shard_map/dot_general | solution.py:36
  459.6 12.3 %copy.17 = bf16[2048,2048]{1,0:T(8,128)(2,1)} copy(bf16[2048,2048]{0,1:T(8,128)(2,1)} %fusion.1) | data formatting | bytes 16777216
  471.9 1.8 convert_element_type.71
  473.7 43.7 %reduce-scatter.11.cloned.1.call-done = f32[64,2048]{1,0:T(8,128)} async-done(((f32[512,2048]{1,0:T(8,128)}), f32[64,2048]{1,0:T(8,128)}) %reduce-scatter.11.cloned.1.call-update) | async-done | bytes 524304 | tf_op jit(solution)/shard_map/reduce_scatter | solution.py:86
  517.3 1.8 convert_element_type.74
  (31 shorter events, 0.5 us)
Async XLA Ops:
  7.2 33.2 %all-gather.7.cloned.1.call-start = ((), (), s32[]{:S(2)}) async-start(), calls=%async_computation.7 | async-start | bytes 2359296 | tf_op jit(solution)/shard_map/all_gather | solution.py:67
  7.9 82.0 %all-gather.5.cloned.1.call-start = ((), (), s32[]{:S(2)}) async-start(), calls=%async_computation.4 | async-start | bytes 2359296 | tf_op jit(solution)/shard_map/all_gather | solution.py:48
  8.7 140.6 %reduce-scatter.9.cloned.1.call-start = ((), (), s32[]{:S(2)}) async-start(), calls=%async_computation.8 | async-start | bytes 5242880 | tf_op jit(solution)/shard_map/reduce_scatter | solution.py:72
  50.9 0.7 copy-start.3
  50.9 245.6 %reduce-scatter.5.cloned.1.call-start = ((), (), s32[]{:S(2)}) async-start(), calls=%async_computation.5 | async-start | bytes 10485760 | tf_op jit(solution)/shard_map/reduce_scatter | solution.py:52
  89.9 7.8 %copy-start = (bf16[2048,2048]{0,1:T(8,128)(2,1)S(1)}, bf16[2048,2048]{0,1:T(8,128)(2,1)}, u32[]{:S(2)}) copy-start(bf16[2048,2048]{0,1:T(8,128)(2,1)} %get-tuple-element.13) | copy-start | bytes 25165828
  89.9 7.8 %copy-start.4 = (bf16[512,2048]{1,0:T(8,128)(2,1)S(1)}, bf16[512,2048]{1,0:T(8,128)(2,1)}, u32[]{:S(2)}) copy-start(bf16[512,2048]{1,0:T(8,128)(2,1)} %all-gather.5.cloned.1.call-done) | copy-start | bytes 6291460
  106.8 277.7 %all-gather.9.cloned.1.call-start = ((), (), s32[]{:S(2)}) async-start(), calls=%async_computation.9 | async-start | bytes 2621440 | tf_op jit(solution)/shard_map/all_gather | solution.py:80
  300.0 110.0 %all-gather.11.cloned.1.call-start = ((), (), s32[]{:S(2)}) async-start(), calls=%async_computation.10 | async-start | bytes 2621440 | tf_op jit(solution)/shard_map/all_gather | solution.py:81
  300.1 18.9 %collective-permute-start = (bf16[128,2048]{0,1:T(8,128)(2,1)S(1)}, bf16[128,2048]{0,1:T(8,128)(2,1)S(1)}, u32[]{:S(2)}, u32[]{:S(2)}) collective-permute-start(bf16[128,2048]{0,1:T(8,128)(2,1)S(1)} %get-tuple-element.12), channel_id=1, source_target_pairs={{0,8},{8,16},{16,24},{24,0},{1,9},{9,17},{17,25},{25,1},{2,10},{10... | collective-permute-start | bytes 1572872 | tf_op jit(solution)/shard_map/ppermute | solution.py:16
  319.0 28.9 %collective-permute-start.1 = (bf16[128,2048]{0,1:T(8,128)(2,1)S(1)}, bf16[128,2048]{0,1:T(8,128)(2,1)S(1)}, u32[]{:S(2)}, u32[]{:S(2)}) collective-permute-start(bf16[128,2048]{0,1:T(8,128)(2,1)S(1)} %collective-permute-done), channel_id=1, source_target_pairs={{0,8},{8,16},{16,24},{24,0},{1,9},{9,17},{17,25},{25,1},{2,10},{10... | collective-permute-start | bytes 1572872 | tf_op jit(solution)/shard_map/ppermute | solution.py:16
  347.8 23.6 %collective-permute-start.2 = (bf16[128,2048]{0,1:T(8,128)(2,1)S(1)}, bf16[128,2048]{0,1:T(8,128)(2,1)S(1)}, u32[]{:S(2)}, u32[]{:S(2)}) collective-permute-start(bf16[128,2048]{0,1:T(8,128)(2,1)S(1)} %collective-permute-done.1), channel_id=1, source_target_pairs={{0,8},{8,16},{16,24},{24,0},{1,9},{9,17},{17,25},{25,1},{2,10},{10... | collective-permute-start | bytes 1572872 | tf_op jit(solution)/shard_map/ppermute | solution.py:16
  356.4 115.5 %reduce-scatter.7.cloned.1.call-start = ((), (), s32[]{:S(2)}) async-start(), calls=%async_computation.6 | async-start | bytes 4718592 | tf_op jit(solution)/shard_map/reduce_scatter | solution.py:61
  372.9 1.9 copy-start.2
  384.4 132.9 %reduce-scatter.11.cloned.1.call-start = ((), (), s32[]{:S(2)}) async-start(), calls=%async_computation.11 | async-start | bytes 4718592 | tf_op jit(solution)/shard_map/reduce_scatter | solution.py:86
  421.7 1.8 copy-start.6
  423.5 8.6 %copy-start.5 = (bf16[512,2048]{1,0:T(8,128)(2,1)S(1)}, bf16[512,2048]{1,0:T(8,128)(2,1)}, u32[]{:S(2)}) copy-start(bf16[512,2048]{1,0:T(8,128)(2,1)} %all-gather.5.cloned.1.call-done) | copy-start | bytes 6291460
  423.5 8.6 %copy-start.7 = (bf16[512,2048]{0,1:T(8,128)(2,1)S(1)}, bf16[512,2048]{0,1:T(8,128)(2,1)}, u32[]{:S(2)}) copy-start(bf16[512,2048]{0,1:T(8,128)(2,1)} %all-gather.9.cloned.1.call-done) | copy-start | bytes 6291460
  438.9 12.4 %copy-start.1 = (bf16[512,2048]{0,1:T(8,128)(2,1)S(1)}, bf16[512,2048]{0,1:T(8,128)(2,1)}, u32[]{:S(2)}) copy-start(bf16[512,2048]{0,1:T(8,128)(2,1)} %all-gather.11.cloned.1.call-done) | copy-start | bytes 6291460
Sparse Core Ops, SparseCore 0:
  9.9 30.4 all-gather.6
  42.3 27.7 all-gather.4
  72.4 76.7 reduce-scatter.8
  151.4 145.1 reduce-scatter.4
  300.2 63.7 all-gather.8
  365.3 44.6 all-gather.10
  413.4 49.3 reduce-scatter.6
  466.1 51.1 reduce-scatter.10
